TPU v7x, 512 devices: a whole 4x8x8 slice. The times are simulated.
512 devices in a mesh: blk: 16 (over z_lo, y), seq: 32 (over x, z_hi, core).
Axes of the slice: x: 4, y: 8, z: 8 (z_hi: 4, z_lo: 2; z = z_hi * 2 + z_lo), core: 2. Of those that a mesh axis runs over, the one named last changes fastest.
Arguments:
- tokens: bfloat16 [16, 8192, 1024], P('blk', 'seq'), may hold values from -128 to 128
- expert_ids: int32 [16, 8192, 1], P('blk', 'seq'), may hold values from 0 to 31; in each aligned block of 256 rows (0 to 255, 256 to 511, ..., all dimensions but the last counted through in order) at most 16 rows name the same one
- expert_capacity: int32 [32], replicated, may hold values from 8 to 16, as said below
- kernel_weight: bfloat16 [1024, 496], replicated, may hold values from -1 to 1
- norm_gain: bfloat16 [1024], replicated, may hold values from 0.25 to 1.75
- router: bfloat16 [1024, 32], replicated, may hold values from -0.1875 to 0.1875
- expert_gate: bfloat16 [32, 1024, 2048], P('seq', None, 'blk'), may hold values from -0.1875 to 0.1875
- expert_up: bfloat16 [32, 1024, 2048], P('seq', None, 'blk'), may hold values from -0.1875 to 0.1875
- expert_down: bfloat16 [32, 1024, 2048], P('seq', None, 'blk'), may hold values from -0.125 to 0.125
Outputs:
- result: bfloat16 [16, 8192, 1024], P('blk', 'seq')
Inputs may be any that keep to these rules, and one draw needn't show every extreme that they name: `expert_ids`: in each aligned block of 256 positions (the positions of one device) no expert is named more than 16 times, a bound that some block reaches. `expert_capacity`: some expert has capacity exactly 16.
All inputs are finite; a program needn't handle non-finite values.
Results may differ from a plain program's by a relative error of at most 0.004.
Values may be sent and summed in bfloat16 or wider, within the bound.
A program may use at most 128 MiB of HBM per device.

v0:
```python
import jax
import jax.numpy as jnp
from jax import lax
from jax.sharding import PartitionSpec as P

HEADS = 16
TAPS = 31


EPS = 1e-06


def padded_2(block, sides, width):
    for axis, dim in sides:
        count = lax.axis_size(axis)
        forward = [(i, i + 1) for i in range(count - 1)]
        backward = [(target, source) for source, target in forward]
        low = lax.ppermute(
            lax.slice_in_dim(block, block.shape[dim] - width, None, axis=dim), axis, forward
        )
        high = lax.ppermute(lax.slice_in_dim(block, 0, width, axis=dim), axis, backward)
        block = jnp.concatenate([low, block, high], axis=dim)
    return block


def expert_rows(rows, gate_piece, up_piece, down_piece):
    gated = jnp.dot(rows, gate_piece, preferred_element_type=jnp.float32)
    lifted = jnp.dot(rows, up_piece, preferred_element_type=jnp.float32)
    act = (jax.nn.silu(gated) * lifted).astype(jnp.bfloat16)
    return lax.dot_general(
        act, down_piece, (((1,), (1,)), ((), ())), preferred_element_type=jnp.float32
    )


def on_device(
    tokens,
    expert_ids,
    expert_capacity,
    kernel_weight,
    norm_gain,
    router,
    expert_gate,
    expert_up,
    expert_down,
):
    local = tokens[0]
    count, width = local.shape
    head_width = width // HEADS
    padded = padded_2(tokens, (("seq", 1),), TAPS // 2)[0]
    logits = jnp.dot(local, kernel_weight, preferred_element_type=jnp.float32).reshape(
        count, HEADS, TAPS
    )
    probs = jax.nn.softmax(logits, axis=-1).astype(jnp.bfloat16)
    mixed = local.astype(jnp.float32)
    for k in range(TAPS):
        weight = jnp.repeat(probs[:, :, k].astype(jnp.float32), head_width, axis=1)
        mixed = mixed + weight * padded[k : k + count].astype(jnp.float32)
    scale = lax.rsqrt(jnp.mean(mixed * mixed, axis=-1, keepdims=True) + EPS)
    normed = (mixed * scale * norm_gain.astype(jnp.float32)).astype(jnp.bfloat16)
    experts = expert_capacity.shape[0]
    depth = max(2, 2 * count // experts)
    ids = expert_ids[0, :, 0]
    onehot = (ids[:, None] == jnp.arange(experts, dtype=jnp.int32)[None, :]).astype(jnp.int32)
    rank = jnp.sum((jnp.cumsum(onehot, axis=0) - 1) * onehot, axis=1)
    limit = jnp.sum(onehot * expert_capacity[None, :], axis=1)
    kept = rank < limit
    slot = jnp.where(kept, ids * depth + rank, -1)
    select = (slot[:, None] == jnp.arange(experts * depth, dtype=jnp.int32)[None, :]).astype(
        jnp.bfloat16
    )
    gate_all = jnp.dot(normed, router, preferred_element_type=jnp.float32)
    gate = jax.nn.sigmoid(jnp.sum(gate_all * onehot.astype(jnp.float32), axis=1))
    packed = lax.dot_general(
        select, normed, (((0,), (0,)), ((), ())), preferred_element_type=jnp.float32
    )
    packed = packed.astype(jnp.bfloat16).reshape(experts, depth, width)
    arrived = lax.all_to_all(packed, "seq", split_axis=0, concat_axis=0, tiled=True)
    rows = arrived.reshape(-1, width)
    produced = expert_rows(
        rows,
        lax.all_gather(expert_gate, "blk", axis=2, tiled=True)[0],
        lax.all_gather(expert_up, "blk", axis=2, tiled=True)[0],
        lax.all_gather(expert_down, "blk", axis=2, tiled=True)[0],
    )
    sent = produced.astype(jnp.bfloat16).reshape(arrived.shape)
    back = lax.all_to_all(sent, "seq", split_axis=0, concat_axis=0, tiled=True).reshape(
        experts * depth, width
    )
    token_out = jnp.dot(select, back, preferred_element_type=jnp.float32)
    result = mixed + gate[:, None] * token_out
    return result.astype(jnp.bfloat16)[None]


def solution(mesh):
    placed = (
        P("blk", "seq", None),
        P("blk", "seq", None),
        P(),
        P(),
        P(),
        P(),
        P("seq", None, "blk"),
        P("seq", None, "blk"),
        P("seq", None, "blk"),
    )
    return jax.shard_map(
        on_device, mesh=mesh, in_specs=placed, out_specs=P("blk", "seq", None), check_vma=False
    )
```

profile of v0, /device:TPU:1, one launch (start us, length us, event | category | flops | bytes accessed | tf_op | source)
XLA Modules:
  0.0 349.5 jit_solution(1133821033578484074)
XLA Ops:
  6.6 0.7 all-gather.4.cloned.1.call-update
  7.3 0.7 all-gather.6.cloned.1.call-update
  8.1 1.4 fusion.90
  9.5 8.8 %collective-permute-start.1 = (bf16[1,15,1024]{2,1,0:T(8,128)(2,1)}, bf16[1,15,1024]{2,1,0:T(8,128)(2,1)}, u32[]{:S(2)}, u32[]{:S(2)}) collective-permute-start(bf16[1,15,1024]{2,1,0:T(8,128)(2,1)} %get-tuple-element.10), channel_id=1, source_target_pairs={{1,0},{2,1},{3,2},{4,3},{5,4},{6,5},{7,6},{8,7},{9,8},{10,9},{11,1... | collective-permute-start | bytes 92168 | tf_op jit(solution)/shard_map/ppermute | solution.py:21
  18.3 1.9 collective-permute-start
  20.2 1.5 dot_general.26
  21.7 1.6 fusion.91
  23.4 0.9 slice_convert_fusion.30
  24.3 0.6 reduce-window.6
  25.1 0.6 copy_bitcast_fusion.16
  25.7 0.6 copy_bitcast_fusion.14
  26.3 0.6 copy_bitcast_fusion.12
  26.9 0.6 copy_bitcast_fusion.10
  27.6 0.6 compare_select_fusion
  28.2 0.6 copy_bitcast_fusion.4
  29.0 0.6 copy_bitcast_fusion.28
  30.2 0.8 broadcast_in_dim.123
  31.0 1.4 copy.56
  32.3 0.8 broadcast_in_dim.124
  33.1 1.3 copy.57
  34.4 0.8 broadcast_in_dim.125
  35.2 1.3 copy.58
  36.6 0.8 broadcast_in_dim.126
  37.4 1.3 copy.59
  38.7 0.8 broadcast_in_dim.127
  39.5 1.3 copy.60
  40.8 0.8 broadcast_in_dim.128
  41.6 1.3 copy.61
  42.9 0.8 broadcast_in_dim.129
  43.7 1.3 copy.62
  45.1 1.4 copy.63
  46.6 1.3 copy.64
  48.0 1.3 copy.65
  49.4 1.3 copy.66
  50.8 1.4 copy.67
  52.3 1.3 copy.68
  53.7 1.3 copy.69
  55.1 1.3 copy.70
  56.5 1.4 copy.71
  58.0 1.4 copy.72
  59.4 1.3 copy.43
  60.8 1.3 copy.44
  62.2 1.4 copy.45
  63.7 1.3 copy.46
  65.1 1.3 copy.47
  66.4 1.3 copy.48
  67.9 1.4 copy.49
  69.3 1.3 copy.50
  70.7 1.3 copy.51
  72.1 1.3 copy.52
  73.6 1.3 copy.53
  75.0 1.3 copy.54
  76.4 1.4 copy.42
  77.8 0.8 constant_dynamic-update-slice_fusion
  78.6 13.5 %multiply_reduce_fusion = (f32[256]{0:T(256)S(1)}, f32[256,1024]{1,0:T(8,128)S(1)}) fusion(f32[256,1024]{1,0:T(8,128)} %copy.72, bf16[1,271,1024]{2,1,0:T(8,128)(2,1)S(1)} %constant_dynamic-update-slice_fusion, f32[256,1024]{1,0:T(8,128)} %copy.71, f32[256,1024]{1,0:T(8,128)} %copy.70, f32[256,1024]{1,0:T(8,128)} %copy.69, f32[256,1024]{1,0:T(8,128)} %copy.68, ...), kind=kLoop, calls=%fused_computation.95 | loop fusion | flops 40632064 | bytes 41974784 | tf_op jit(solution)/shard_map/reduce_sum | solution.py:58
  92.1 0.6 convolution_convert_fusion
  92.7 36.5 %all_to_all.10 = bf16[32,16,1024]{2,1,0:T(8,128)(2,1)S(1)} all-to-all(bf16[32,16,1024]{2,1,0:T(8,128)(2,1)S(1)} %bitcast.328), channel_id=1, replica_groups=mesh['blk'=16,'seq'=32] {'seq'}, dimensions={0} | all-to-all | bytes 2097152 | tf_op jit(solution)/shard_map/all_to_all | solution.py:77
  129.1 6.5 %fusion.5 = f32[512,2048]{1,0:T(8,128)} fusion(bf16[512,1024]{1,0:T(8,128)(2,1)S(1)} %bitcast.361, bf16[1,1024,2048]{2,1,0:T(8,128)(2,1)} %all-gather.4.cloned.1.call-done), kind=kOutput, calls=%fused_computation.5 | convolution fusion | flops 2147483648 | bytes 9437184 | tf_op jit(solution)/shard_map/dot_general | solution.py:27
  135.7 55.3 %all-gather.6.cloned.1.call-done = bf16[1,1024,2048]{2,1,0:T(8,128)(2,1)} async-done(((bf16[1,1024,128]{2,1,0:T(8,128)(2,1)}), bf16[1,1024,2048]{2,1,0:T(8,128)(2,1)}) %all-gather.6.cloned.1.call-update) | async-done | bytes 4194320 | tf_op jit(solution)/shard_map/all_gather | solution.py:82
  190.9 92.6 %all-gather.8.cloned.1.call-done = bf16[1,1024,2048]{2,1,0:T(8,128)(2,1)} async-done(((bf16[1,1024,128]{2,1,0:T(8,128)(2,1)}), bf16[1,1024,2048]{2,1,0:T(8,128)(2,1)}) %all-gather.8.cloned.1.call-update) | async-done | bytes 4194320 | tf_op jit(solution)/shard_map/all_gather | solution.py:83
  283.5 10.2 %fusion.11 = bf16[512,1024]{1,0:T(8,128)(2,1)} fusion(bf16[1,1024,2048]{2,1,0:T(8,128)(2,1)} %all-gather.8.cloned.1.call-done, f32[512,2048]{1,0:T(8,128)} %fusion.5, bf16[512,1024]{1,0:T(8,128)(2,1)S(1)} %bitcast.362, bf16[1,1024,2048]{2,1,0:T(8,128)(2,1)} %all-gather.6.cloned.1.call-done), kind=kOutput, calls=%fused_computation.23 | convolution fusion | flops 4301783040 | bytes 14680064 | tf_op jit(solution)/shard_map/dot_general | solution.py:30
  293.7 19.6 %all-to-all-start.1 = ((bf16[32,16,1024]{2,1,0:T(8,128)(2,1)}), bf16[32,16,1024]{2,1,0:T(8,128)(2,1)S(1)}, u32[]{:S(2)}, u32[]{:S(2)}) async-start(bf16[32,16,1024]{2,1,0:T(8,128)(2,1)} %bitcast.363), calls=%async_computation.1 | async-start | bytes 2097152 | tf_op jit(solution)/shard_map/all_to_all | solution.py:86
  313.7 28.0 %all-to-all-done.1 = bf16[32,16,1024]{2,1,0:T(8,128)(2,1)S(1)} async-done(((bf16[32,16,1024]{2,1,0:T(8,128)(2,1)}), bf16[32,16,1024]{2,1,0:T(8,128)(2,1)S(1)}, u32[]{:S(2)}, u32[]{:S(2)}) %all-to-all-start.1) | async-done | bytes 1048608 | tf_op jit(solution)/shard_map/all_to_all | solution.py:86
  341.7 1.3 fusion.20
  (76 shorter events, 3.3 us)
Async XLA Ops:
  6.5 306.8 %copy-start = (bf16[1024,32]{0,1:T(8,128)(2,1)S(1)}, bf16[1024,32]{0,1:T(8,128)(2,1)}, u32[]{:S(2)}) copy-start(bf16[1024,32]{0,1:T(8,128)(2,1)} %param.14) | copy-start | bytes 196612
  6.5 23.1 %copy-start.1 = (bf16[1,256,1024]{2,1,0:T(8,128)(2,1)S(1)}, bf16[1,256,1024]{2,1,0:T(8,128)(2,1)}, u32[]{:S(2)}) copy-start(bf16[1,256,1024]{2,1,0:T(8,128)(2,1)} %param.9) | copy-start | bytes 1572868
  6.5 17.7 %copy-start.6 = (s32[1,256,1]{1,2,0:T(1,128)S(1)}, s32[1,256,1]{1,2,0:T(1,128)}, u32[]{:S(2)}) copy-start(s32[1,256,1]{1,2,0:T(1,128)} %param.10) | copy-start | bytes 3076
  6.5 21.0 %copy-start.10 = (s32[32]{0:T(128)S(1)}, s32[32]{0:T(128)}, u32[]{:S(2)}) copy-start(s32[32]{0:T(128)} %param.11) | copy-start | bytes 388
  6.5 122.6 %all-gather.4.cloned.1.call-start = ((), (), s32[]{:S(2)}) async-start(), calls=%async_computation.2 | async-start | bytes 4456448 | tf_op jit(solution)/shard_map/all_gather | solution.py:81
  7.3 183.6 %all-gather.6.cloned.1.call-start = ((), (), s32[]{:S(2)}) async-start(), calls=%async_computation.3 | async-start | bytes 4456448 | tf_op jit(solution)/shard_map/all_gather | solution.py:82
  8.0 275.5 %all-gather.8.cloned.1.call-start = ((), (), s32[]{:S(2)}) async-start(), calls=%async_computation.4 | async-start | bytes 4456448 | tf_op jit(solution)/shard_map/all_gather | solution.py:83
  9.5 68.3 %collective-permute-start.1 = (bf16[1,15,1024]{2,1,0:T(8,128)(2,1)}, bf16[1,15,1024]{2,1,0:T(8,128)(2,1)}, u32[]{:S(2)}, u32[]{:S(2)}) collective-permute-start(bf16[1,15,1024]{2,1,0:T(8,128)(2,1)} %get-tuple-element.10), channel_id=1, source_target_pairs={{1,0},{2,1},{3,2},{4,3},{5,4},{6,5},{7,6},{8,7},{9,8},{10,9},{11,1... | collective-permute-start | bytes 92168 | tf_op jit(solution)/shard_map/ppermute | solution.py:21
  18.3 60.3 %collective-permute-start = (bf16[1,15,1024]{2,1,0:T(8,128)(2,1)}, bf16[1,15,1024]{2,1,0:T(8,128)(2,1)}, u32[]{:S(2)}, u32[]{:S(2)}) collective-permute-start(bf16[1,15,1024]{2,1,0:T(8,128)(2,1)} %get-tuple-element.9), channel_id=1, source_target_pairs={{0,1},{1,2},{2,3},{3,4},{4,5},{5,6},{6,7},{7,8},{8,9},{9,10},{10,1... | collective-permute-start | bytes 92168 | tf_op jit(solution)/shard_map/ppermute | solution.py:18
  46.6 4.1 %copy-start.3 = (f32[256,16]{0,1:T(8,128)S(1)}, f32[256,16]{0,1:T(8,128)}, u32[]{:S(2)}) copy-start(f32[256,16]{0,1:T(8,128)} %get-tuple-element.49) | copy-start | bytes 49156
  55.1 4.3 %copy-start.4 = (f32[256,16]{0,1:T(8,128)S(1)}, f32[256,16]{0,1:T(8,128)}, u32[]{:S(2)}) copy-start(f32[256,16]{0,1:T(8,128)} %get-tuple-element.73) | copy-start | bytes 49156
  56.5 4.2 %copy-start.2 = (f32[256,16]{0,1:T(8,128)S(1)}, f32[256,16]{0,1:T(8,128)}, u32[]{:S(2)}) copy-start(f32[256,16]{0,1:T(8,128)} %get-tuple-element.72) | copy-start | bytes 49156
  72.1 4.2 %copy-start.5 = (f32[256,16,1]{0,2,1:T(1,128)S(1)}, f32[256,16,1]{0,2,1:T(1,128)}, u32[]{:S(2)}) copy-start(f32[256,16,1]{0,2,1:T(1,128)} %get-tuple-element.11) | copy-start | bytes 49156
  73.5 4.2 %copy-start.9 = (bf16[1024]{0:T(1024)(128)(2,1)S(1)}, bf16[1024]{0:T(1024)(128)(2,1)}, u32[]{:S(2)}) copy-start(bf16[1024]{0:T(1024)(128)(2,1)} %param.13) | copy-start | bytes 6148
  78.6 13.5 %copy-start.8 = (s32[256]{0:T(256)S(1)}, s32[256]{0:T(256)}, u32[]{:S(2)}) copy-start(s32[256]{0:T(256)} %compare_select_fusion) | copy-start | bytes 3076
  135.7 177.6 %copy-start.7 = (s32[1,256,1]{1,2,0:T(1,128)S(1)}, s32[1,256,1]{1,2,0:T(1,128)}, u32[]{:S(2)}) copy-start(s32[1,256,1]{1,2,0:T(1,128)} %param.10) | copy-start | bytes 3076
  293.7 48.0 %all-to-all-start.1 = ((bf16[32,16,1024]{2,1,0:T(8,128)(2,1)}), bf16[32,16,1024]{2,1,0:T(8,128)(2,1)S(1)}, u32[]{:S(2)}, u32[]{:S(2)}) async-start(bf16[32,16,1024]{2,1,0:T(8,128)(2,1)} %bitcast.363), calls=%async_computation.1 | async-start | bytes 2097152 | tf_op jit(solution)/shard_map/all_to_all | solution.py:86
Sparse Core Ops, SparseCore 0:
  9.4 87.8 all-gather.3
  99.2 91.6 all-gather.5
  192.9 90.5 all-gather.7
where the time goes:
time: 350 us; the launch traced here: 349 us
  waiting for transfers between devices  177 us (51%)
  local copies, waits for them, and re-layouts  55.4 us (16%)
  blocking collectives  36.5 us (10%)
  starting transfers between devices  30.4 us (9%)
  matrix products  20.5 us (6%)
  other arithmetic  15.9 us (5%)
  between operations  13.6 us (4%)
    all_gather x1, waiting for transfers between devices, on_device(): lax.all_gather(expert_down, 'blk', axis=2, tiled=True)[0]  92.6 us
    all_gather x1, waiting for transfers between devices, on_device(): lax.all_gather(expert_up, 'blk', axis=2, tiled=True)[0]  55.3 us
    reshape x31, local copies, waits for them, and re-layouts, on_device(): weight = jnp.repeat(probs[:, :, k].astype(jnp.float32), head_width, axis=1)  40.4 us
    all_to_all x1, blocking collectives, on_device(): lax.all_to_all(packed, 'seq', split_axis=0, concat_axis=0, tiled=True)  36.5 us
    all_to_all x1, waiting for transfers between devices, on_device(): lax.all_to_all(sent, 'seq', split_axis=0, concat_axis=0, tiled=True)  28 us
    all_to_all x1, starting transfers between devices, on_device(): lax.all_to_all(sent, 'seq', split_axis=0, concat_axis=0, tiled=True)  19.6 us
    reduce_sum x1, other arithmetic, on_device(): scale = lax.rsqrt(jnp.mean(mixed * mixed, axis=-1, keepdims=True) + EPS)  13.5 us
    dot_general x1, matrix products, expert_rows(): lax.dot_general(act, down_piece, (((1,), (1,)), ((), ())), preferred_elem...  10.2 us
  transfers between devices with their start and end apart: 6, of which 3 were waited for; matrix products, arithmetic and copies ran while one was open for 23% of the time, Pallas kernels for 0%

commit v1 on v0

v1 whole, which is shorter than its diff:
```python
import functools

import jax
import jax.numpy as jnp
from jax import lax
from jax.experimental import pallas as pl
from jax.experimental.pallas import tpu as pltpu
from jax.sharding import PartitionSpec as P

MESH = pl.DeviceIdType.MESH
F32 = jnp.float32
BF16 = jnp.bfloat16

D = 1024
HEADS = 16
TAPS = 31
HALF = 15
TOK = 256
EXPERTS = 32
CAP = 16
SLOTS = EXPERTS * CAP
EPS = 1e-06

NX, NH, NC, NY = 4, 4, 2, 8
GROUP = NX * NC * CAP
PIECE = 128
PARTS = 2
FEAT = D // PARTS

OWN, FAR = 0, 7
LEFT = (0, 1, 2, 3, 7)
RIGHT = (0, 4, 5, 6, 7)
ORDER = (0, 1, 4, 2, 5, 3, 6, 7)


def dot(a, b):
    return jnp.dot(a, b, preferred_element_type=F32)


def dot_nt(a, b):
    return lax.dot_general(a, b, (((1,), (1,)), ((), ())), preferred_element_type=F32)


def iota(shape, dim):
    return lax.broadcasted_iota(jnp.int32, shape, dim)


def layer(
    tokens, idc, idr, capc, capr, kwt, gain, router, gate_w, up_w, down_w,
    out,
    xp, pt, mixed, normed, packed, sel, gate_s,
    rows, gu, wd, act, ps, pr, mine, bs, bk,
    local_sem, halo_s, halo_r, ag_s, ag_r, fwd_s, fwd_r, ex_s, ex_r, px_s, px_r, ret_s, ret_r,
):
    s = lax.axis_index("seq")
    b = lax.axis_index("blk")
    lo, y = b // NY, lax.rem(b, NY)
    c = lax.rem(s, NC)
    h = lax.rem(s // NC, NH)
    x = s // (NC * NH)
    right = lo * NY + lax.rem(y + 1, NY)
    left = lo * NY + lax.rem(y + NY - 1, NY)
    pair = (1 - lo) * NY + y
    seqs = NX * NH * NC

    barrier = pltpu.get_barrier_semaphore()

    def greet(i, _):
        t = lax.rem(s + i, seqs)
        for other in range(2):
            pl.semaphore_signal(barrier, inc=1, device_id=(other * NY + y, t), device_id_type=MESH)
        return 0

    lax.fori_loop(1, seqs, greet, 0)
    for t in (pair, left, right):
        pl.semaphore_signal(barrier, inc=1, device_id=(t, s), device_id_type=MESH)
    pl.semaphore_wait(barrier, 2 * (seqs - 1) + 3)

    def remote(src, dst, ss, rs, blk, seq):
        return pltpu.make_async_remote_copy(
            src_ref=src, dst_ref=dst, send_sem=ss, recv_sem=rs, device_id=(blk, seq), device_id_type=MESH
        )

    def g_view(slot):
        return gu.at[slot, :, pl.ds(0, PIECE)]

    def u_view(slot):
        return gu.at[slot, :, pl.ds(PIECE, PIECE)]

    def d_view(slot):
        return wd.at[:, pl.ds(slot * PIECE, PIECE)]

    def d_half(slot, half):
        return wd.at[pl.ds(half * (D // 2), D // 2), pl.ds(slot * PIECE, PIECE)]

    views = (g_view, u_view, d_view)
    args = (gate_w.at[0], up_w.at[0], down_w.at[0])

    def hop(way, step, a):
        slots = (LEFT, RIGHT)[way]
        target = (right, left)[way]
        sems = ag_s.at[way, step - 1, a], ag_r.at[way, step - 1, a]
        if step == 4 and a == 2:
            src, dst = d_half(slots[3], way), d_half(FAR, way)
        elif step == 1:
            src, dst = args[a], views[a](slots[1])
        else:
            src, dst = views[a](slots[step - 1]), views[a](slots[step])
        return remote(src, dst, *sems, target, s)

    hops = []

    def send(step, a):
        for way in range(2):
            if step == 4 and a < 2 and a != way:
                continue
            cp = hop(way, step, a)
            cp.start()
            hops.append(cp)

    def forward(step, a):
        for way in range(2):
            hop(way, step, a).wait_recv()
            if step < 3 or a == 2 or a == way:
                cp = hop(way, step + 1, a)
                cp.start()
                hops.append(cp)

    tail = remote(tokens.at[0, pl.ds(TOK - CAP, CAP)], xp.at[pl.ds(0, CAP)], halo_s.at[0], halo_r.at[0], b, lax.rem(s + 1, seqs))
    head = remote(tokens.at[0, pl.ds(0, CAP)], xp.at[pl.ds(TOK + CAP, CAP)], halo_s.at[1], halo_r.at[1], b, lax.rem(s + seqs - 1, seqs))
    tail.start()
    head.start()
    send(1, 0)
    send(1, 1)
    locals_ = [
        pltpu.make_async_copy(args[a], views[a](OWN), local_sem.at[a]) for a in range(3)
    ]
    for cp in locals_:
        cp.start()

    xp[pl.ds(CAP, TOK)] = tokens[0]
    xp[pl.ds(TOK + 2 * CAP, 32)] = jnp.zeros((32, D), BF16)
    row, col = iota((512, HEADS * TAPS), 0), iota((512, HEADS * TAPS), 1)
    tap = row & 31
    spread = ((col == (row >> 5) * TAPS + tap) & (tap < TAPS)).astype(F32).astype(BF16)
    kw = dot(spread, kwt[...]).astype(BF16)
    for q in range(4):
        logits = dot_nt(kw[q * 128 : (q + 1) * 128], tokens[0]).reshape(4, 32, TOK)
        logits = jnp.where(iota(logits.shape, 1) < TAPS, logits, -3e38)
        e = jnp.exp(logits - jnp.max(logits, axis=1, keepdims=True))
        p = e / jnp.sum(e, axis=1, keepdims=True)
        pt[q] = p.astype(BF16).astype(F32).reshape(128, TOK).T

    tail.wait_recv()
    head.wait_recv()
    first, last = (s > 0).astype(F32), (s < seqs - 1).astype(F32)
    xp[pl.ds(0, CAP)] = (xp[pl.ds(0, CAP)].astype(F32) * first).astype(BF16)
    xp[pl.ds(TOK + CAP, CAP)] = (xp[pl.ds(TOK + CAP, CAP)].astype(F32) * last).astype(BF16)

    lane = iota((64, 128), 1)
    for q in range(4):
        for t in range(TOK // 64):
            p = pt[q, pl.ds(t * 64, 64)]
            bands = []
            for i in range(4):
                mine_only = jnp.where((lane >> 5) == i, p, 0.0)
                bands.append(
                    pltpu.roll(mine_only, (1 - 32 * i) % 128, 1, stride=1, stride_axis=0).astype(BF16)
                )
            for i in range(2):
                cols = pl.ds((2 * q + i) * 128, 128)
                window = xp[pl.ds(t * 64, 128), cols]
                conv = jnp.where(lane < 64, dot(bands[2 * i], window), dot(bands[2 * i + 1], window))
                mixed[pl.ds(t * 64, 64), cols] = conv + tokens[0, pl.ds(t * 64, 64), cols].astype(F32)

    m = mixed[...]
    scale = lax.rsqrt(jnp.mean(m * m, axis=1, keepdims=True) + EPS)
    normed[...] = (m * scale * gain[...].astype(F32)).astype(BF16)
    one_c = idc[...] == iota((TOK, EXPERTS), 1)
    one_r = idr[...] == iota((EXPERTS, TOK), 0)
    fc, fr = one_c.astype(F32), one_r.astype(F32)
    up_tri = (iota((TOK, TOK), 0) < iota((TOK, TOK), 1)).astype(F32).astype(BF16)
    lo_tri = (iota((TOK, TOK), 0) > iota((TOK, TOK), 1)).astype(F32).astype(BF16)
    rank_c = jnp.sum(dot(lo_tri, fc.astype(BF16)) * fc, axis=1, keepdims=True)
    rank_r = jnp.sum(dot(fr.astype(BF16), up_tri) * fr, axis=0, keepdims=True)
    cap_c = jnp.sum(fc * capr[...].astype(F32), axis=1, keepdims=True)
    cap_r = jnp.sum(fr * capc[...].astype(F32), axis=0, keepdims=True)
    slot_c = jnp.where(rank_c < cap_c, idc[...].astype(F32) * CAP + rank_c, -1.0)
    slot_r = jnp.where(rank_r < cap_r, idr[...].astype(F32) * CAP + rank_r, -1.0)
    sel[...] = (slot_c == iota((TOK, SLOTS), 1).astype(F32)).astype(F32).astype(BF16)
    sel_t = (slot_r == iota((SLOTS, TOK), 0).astype(F32)).astype(F32).astype(BF16)
    chosen = jnp.sum(dot_nt(normed[...], router[...]) * fc, axis=1, keepdims=True)
    gate_s[...] = 1.0 / (1.0 + jnp.exp(-chosen))
    packed[...] = dot(sel_t, normed[...]).astype(BF16)

    place = (x * NC + c) * CAP

    def aligned(v):
        return pl.multiple_of(v, CAP)

    def home(dh):
        return ((lo, 0), (0, 1 + lo), (1 - lo, 3), (1, 1 + lo))[dh]

    for dh in (2, 1, 3, 0):
        home_lo, kind = home(dh)
        to_h = lax.rem(h + dh, NH)

        def to(i, _, home_lo=home_lo, kind=kind, to_h=to_h):
            tx, tc = lax.rem(x + i // NC, NX), lax.rem(c + lax.rem(i, NC), NC)
            e = (tx * NH + to_h) * NC + tc
            remote(
                packed.at[pl.ds(aligned(e * CAP), CAP)],
                rows.at[pl.ds(aligned(kind * GROUP + place), CAP)],
                fwd_s, fwd_r.at[kind], home_lo * NY + y, e,
            ).start()
            return 0

        lax.fori_loop(1 if dh == 0 else 0, NX * NC, to, 0)
    rows[pl.ds(aligned(place), CAP)] = packed[pl.ds(aligned(s * CAP), CAP)]

    send(1, 2)
    forward(1, 0)
    forward(1, 1)

    ex = []

    def exchange(kind):
        n = GROUP - CAP if kind == 0 else GROUP
        block = rows.at[pl.ds(0, n)]
        remote(block, block, fwd_s, fwd_r.at[kind], b, s).wait_recv()
        src = rows.at[pl.ds(kind * GROUP, GROUP)]
        dst = rows.at[pl.ds(SLOTS + kind * GROUP, GROUP)]
        cp = remote(src, dst, ex_s.at[kind], ex_r.at[kind], pair, s)
        cp.start()
        ex.append(cp)

    exchange(0)
    forward(1, 2)
    forward(2, 0)
    forward(2, 1)
    exchange(1)
    exchange(2)
    exchange(3)
    forward(2, 2)
    for cp in locals_:
        cp.wait()

    def units(slot):
        def body(i, _):
            r = pl.ds(pl.multiple_of(i * 256, 256), 256)
            v = dot(rows[r], gu[slot])
            g, u = v[:, :PIECE], v[:, PIECE:]
            act[r, pl.ds(slot * PIECE, PIECE)] = (g / (1.0 + jnp.exp(-g)) * u).astype(BF16)
            return 0

        lax.fori_loop(0, 2 * SLOTS // 256, body, 0)

    for cp in ex:
        cp.wait_recv()
    units(0)
    forward(3, 0)
    forward(3, 1)
    for slot in (1, 4, 2, 5, 3, 6):
        units(slot)
    forward(3, 2)
    hop(0, 4, 0).wait_recv()
    hop(1, 4, 1).wait_recv()
    units(7)
    hop(0, 4, 2).wait_recv()
    hop(1, 4, 2).wait_recv()

    px = []
    for j in range(PARTS):
        def down(i, _, j=j):
            r = pl.ds(pl.multiple_of(i * 256, 256), 256)
            r2 = pl.ds(pl.multiple_of(SLOTS + i * 256, 256), 256)
            ps[j, r] = dot_nt(act[r2], wd[pl.ds(j * FEAT, FEAT)]).astype(BF16)
            return 0

        lax.fori_loop(0, SLOTS // 256, down, 0)
        cp = remote(ps.at[j], pr.at[j], px_s.at[j], px_r.at[j], pair, s)
        cp.start()
        px.append(cp)

    for j in range(PARTS):
        def down_own(i, _, j=j):
            r = pl.ds(pl.multiple_of(i * 256, 256), 256)
            mine[j, r] = dot_nt(act[r], wd[pl.ds(j * FEAT, FEAT)])
            return 0

        lax.fori_loop(0, SLOTS // 256, down_own, 0)

    for j in range(PARTS):
        px[j].wait_recv()
        bs[j] = (mine[j] + pr[j].astype(F32)).astype(BF16)
        near = lax.rem(h + NH - 1 + 2 * lo, NH)
        for kind in (3, 1, 2, 0):
            to_h = (h, near, near, lax.rem(h + 2, NH))[kind]
            to_lo = (lo, 0, 1, 1 - lo)[kind]

            def back(i, _, kind=kind, to_h=to_h, to_lo=to_lo, j=j):
                tx, tc = lax.rem(x + i // NC, NX), lax.rem(c + lax.rem(i, NC), NC)
                t = (tx * NH + to_h) * NC + tc
                remote(
                    bs.at[j, pl.ds(aligned(kind * GROUP + (tx * NC + tc) * CAP), CAP)],
                    bk.at[j, pl.ds(aligned(s * CAP), CAP)],
                    ret_s.at[j], ret_r.at[j], to_lo * NY + y, t,
                ).start()
                return 0

            lax.fori_loop(1 if kind == 0 else 0, NX * NC, back, 0)
        bk[j, pl.ds(aligned(s * CAP), CAP)] = bs[j, pl.ds(aligned(place), CAP)]

    for j in range(PARTS):
        block = bk.at[j, pl.ds(0, SLOTS - CAP)]
        remote(block, block, ret_s.at[j], ret_r.at[j], b, s).wait_recv()
        cols = pl.ds(j * FEAT, FEAT)
        out[0, :, cols] = (mixed[:, cols] + gate_s[...] * dot(sel[...], bk[j])).astype(BF16)

    tail.wait_send()
    head.wait_send()
    for cp in hops + ex + px:
        cp.wait_send()
    block = packed.at[pl.ds(0, SLOTS - CAP)]
    remote(block, block, fwd_s, fwd_r.at[0], b, s).wait_send()
    for j in range(PARTS):
        block = bs.at[j, pl.ds(0, SLOTS - CAP)]
        remote(block, block, ret_s.at[j], ret_r.at[j], b, s).wait_send()


def on_device(tokens, expert_ids, expert_capacity, kernel_weight, norm_gain, router, expert_gate, expert_up, expert_down):
    dma = pltpu.SemaphoreType.DMA
    vmem = pl.BlockSpec(memory_space=pltpu.VMEM)
    anywhere = pl.BlockSpec(memory_space=pl.ANY)
    return pl.pallas_call(
        layer,
        out_shape=jax.ShapeDtypeStruct((1, TOK, D), BF16),
        in_specs=[vmem] * 8 + [anywhere] * 3,
        out_specs=vmem,
        scratch_shapes=[
            pltpu.VMEM((TOK + 4 * CAP, D), BF16),
            pltpu.VMEM((4, TOK, 128), F32),
            pltpu.VMEM((TOK, D), F32),
            pltpu.VMEM((TOK, D), BF16),
            pltpu.VMEM((SLOTS, D), BF16),
            pltpu.VMEM((TOK, SLOTS), BF16),
            pltpu.VMEM((TOK, 1), F32),
            pltpu.VMEM((2 * SLOTS, D), BF16),
            pltpu.VMEM((NY, D, 2 * PIECE), BF16),
            pltpu.VMEM((D, NY * PIECE), BF16),
            pltpu.VMEM((2 * SLOTS, NY * PIECE), BF16),
            pltpu.VMEM((PARTS, SLOTS, FEAT), BF16),
            pltpu.VMEM((PARTS, SLOTS, FEAT), BF16),
            pltpu.VMEM((PARTS, SLOTS, FEAT), F32),
            pltpu.VMEM((PARTS, SLOTS, FEAT), BF16),
            pltpu.VMEM((PARTS, SLOTS, FEAT), BF16),
            dma((3,)),
            dma((2,)), dma((2,)),
            dma((2, 4, 3)), dma((2, 4, 3)),
            dma, dma((4,)),
            dma((4,)), dma((4,)),
            dma((PARTS,)), dma((PARTS,)),
            dma((PARTS,)), dma((PARTS,)),
        ],
        compiler_params=pltpu.CompilerParams(
            collective_id=0, has_side_effects=True, vmem_limit_bytes=56 * 1024 * 1024
        ),
    )(
        tokens,
        expert_ids.reshape(TOK, 1),
        expert_ids.reshape(1, TOK),
        expert_capacity.reshape(EXPERTS, 1),
        expert_capacity.reshape(1, EXPERTS),
        kernel_weight.T,
        norm_gain.reshape(1, D),
        router.T,
        expert_gate,
        expert_up,
        expert_down,
    )


def solution(mesh):
    placed = (
        P("blk", "seq", None),
        P("blk", "seq", None),
        P(),
        P(),
        P(),
        P(),
        P("seq", None, "blk"),
        P("seq", None, "blk"),
        P("seq", None, "blk"),
    )
    return jax.shard_map(
        on_device, mesh=mesh, in_specs=placed, out_specs=P("blk", "seq", None), check_vma=False
    )
```

time: 350 us -> 128 us (0.37)
  waiting for transfers between devices: 177 us -> 0 us
  Pallas kernels: 0 us -> 122 us
  local copies, waits for them, and re-layouts: 55.4 us -> 4.7 us
  blocking collectives: 36.5 us -> 0 us
  starting transfers between devices: 30.4 us -> 0 us
  matrix products: 20.5 us -> 0 us
  other arithmetic: 15.9 us -> 0 us
  between operations: 13.6 us -> 0.01 us
    all_gather x3 -> x0, waiting for transfers between devices: 148 us -> none  [the longest x1 92.6 us: on_device(): lax.all_gather(expert_down, 'blk', axis=2, tiled=True)[0]]
    pallas_call x0 -> x1, Pallas kernels: none -> 122 us  [on_device(): pl.pallas_call(layer, out_shape=jax.ShapeDtypeStruct((1, TOK, D), BF16),...]
    reshape x31 -> x3, local copies, waits for them, and re-layouts: 40.4 us -> 2.08 us  [the longest x1 0.8 us: on_device(): expert_ids.reshape(TOK, 1)]
    all_to_all x1 -> x0, blocking collectives: 36.5 us -> none  [on_device(): lax.all_to_all(packed, 'seq', split_axis=0, concat_axis=0, tiled=True)]
    all_to_all x1 -> x0, waiting for transfers between devices: 28 us -> none  [on_device(): lax.all_to_all(sent, 'seq', split_axis=0, concat_axis=0, tiled=True)]
    all_to_all x1 -> x0, starting transfers between devices: 19.6 us -> none  [on_device(): lax.all_to_all(sent, 'seq', split_axis=0, concat_axis=0, tiled=True)]
    dot_general x5 -> x0, matrix products: 18.9 us -> none  [the longest x1 10.2 us: expert_rows(): lax.dot_general(act, down_piece, (((1,), (1,)), ((), ())), preferred_elem...]
    reduce_sum x2 -> x0, other arithmetic: 13.6 us -> none  [the longest x1 13.5 us: on_device(): scale = lax.rsqrt(jnp.mean(mixed * mixed, axis=-1, keepdims=True) + EPS)]
  transfers between devices with their start and end apart: 6 -> 0, of which waited for: 3 -> 0; matrix products, arithmetic and copies ran while one was open for 23% -> 0% of each run, Pallas kernels for 0% -> 0%
where the time goes in v1:
time: 128 us; the launch traced here: 127 us
  Pallas kernels  122 us (95%)
  local copies, waits for them, and re-layouts  4.7 us (4%)
    pallas_call x1, Pallas kernels, on_device(): pl.pallas_call(layer, out_shape=jax.ShapeDtypeStruct((1, TOK, D), BF16),...  122 us
    unnamed x7, local copies, waits for them, and re-layouts  2.61 us

profile of v1, /device:TPU:1, one launch (start us, length us, event | category | flops | bytes accessed | tf_op | source)
XLA Modules:
  0.0 126.9 jit_solution(10443294137900880370)
XLA Ops:
  0.0 0.0 copy-start.2
  0.0 0.7 copy-done.2
  0.7 0.0 copy-start.1
  0.7 0.6 reshape.19.gain
  1.3 0.1 copy-done.1
  1.3 0.0 copy-start
  1.3 0.7 copy.12.capc
  2.0 0.0 copy-done
  2.0 0.8 copy.11.idc
  2.8 122.2 %shard_map.91 = bf16[1,256,1024]{2,1,0:T(8,128)(2,1)} custom-call(bf16[1,256,1024]{2,1,0:T(8,128)(2,1)} %tokens.1, s32[256,1]{1,0:T(8,128)} %copy.11.idc, s32[1,256]{1,0:T(1,128)} %bitcast.8, s32[32,1]{1,0:T(8,128)} %copy.12.capc, s32[1,32]{1,0:T(1,128)} %bitcast.10, bf16[496,1024]{1,0:T(8,128)(2,1)} %bitcast.6, bf16[1,1024]{1,0:T(2,128)(2,1)} %reshape.19.gain, ...), custom_call_target="tpu_custom_call" | custom-call | tf_op jit(solution)/shard_map/pallas_call | solution.py:335
  125.0 1.9 %copy.14 = bf16[1,256,1024]{2,1,0:T(8,128)(2,1)} copy(bf16[1,256,1024]{2,1,0:T(8,128)(2,1)} %shard_map.91) | data formatting | bytes 1048576
Async XLA Ops:
  0.0 0.7 copy-start.2
  0.7 0.7 copy-start.1
  1.3 0.7 copy-start

commit v2 on v1

--- a/solution.py
+++ b/solution.py
@@ -24,13 +24,16 @@
 NX, NH, NC, NY = 4, 4, 2, 8
 GROUP = NX * NC * CAP
 PIECE = 128
-PARTS = 2
+PARTS = 4
 FEAT = D // PARTS
+BLOCKS = 4
+BLOCK = D // BLOCKS
+HALF_ROWS = SLOTS // 2
+AHEAD = 2
 
 OWN, FAR = 0, 7
 LEFT = (0, 1, 2, 3, 7)
 RIGHT = (0, 4, 5, 6, 7)
-ORDER = (0, 1, 4, 2, 5, 3, 6, 7)
 
 
 def dot(a, b):
@@ -46,7 +49,7 @@
 
 
 def layer(
-    tokens, idc, idr, capc, capr, kwt, gain, router, gate_w, up_w, down_w,
+    tokens, ids, limits, kwt, gain, router, gate_w, up_w, down_w,
     out,
     xp, pt, mixed, normed, packed, sel, gate_s,
     rows, gu, wd, act, ps, pr, mine, bs, bk,
@@ -65,16 +68,16 @@
 
     barrier = pltpu.get_barrier_semaphore()
 
-    def greet(i, _):
-        t = lax.rem(s + i, seqs)
-        for other in range(2):
-            pl.semaphore_signal(barrier, inc=1, device_id=(other * NY + y, t), device_id_type=MESH)
-        return 0
-
-    lax.fori_loop(1, seqs, greet, 0)
+    for dh, to_lo in ((0, lo), (1, lo), (3, lo), (3 - 2 * lo, 1 - lo), (2, 1 - lo)):
+        def greet(i, _, dh=dh, to_lo=to_lo):
+            t = (lax.rem(x + i // NC, NX) * NH + lax.rem(h + dh, NH)) * NC + lax.rem(c + lax.rem(i, NC), NC)
+            pl.semaphore_signal(barrier, inc=1, device_id=(to_lo * NY + y, t), device_id_type=MESH)
+            return 0
+
+        lax.fori_loop(1 if isinstance(dh, int) and dh == 0 else 0, NX * NC, greet, 0)
     for t in (pair, left, right):
         pl.semaphore_signal(barrier, inc=1, device_id=(t, s), device_id_type=MESH)
-    pl.semaphore_wait(barrier, 2 * (seqs - 1) + 3)
+    pl.semaphore_wait(barrier, 5 * NX * NC - 1 + 3)
 
     def remote(src, dst, ss, rs, blk, seq):
         return pltpu.make_async_remote_copy(
@@ -87,33 +90,29 @@
     def u_view(slot):
         return gu.at[slot, :, pl.ds(PIECE, PIECE)]
 
-    def d_view(slot):
-        return wd.at[:, pl.ds(slot * PIECE, PIECE)]
-
-    def d_half(slot, half):
-        return wd.at[pl.ds(half * (D // 2), D // 2), pl.ds(slot * PIECE, PIECE)]
-
-    views = (g_view, u_view, d_view)
-    args = (gate_w.at[0], up_w.at[0], down_w.at[0])
+    def d_view(slot, start, size):
+        return wd.at[pl.ds(start, size), pl.ds(slot * PIECE, PIECE)]
+
+    def view(a, slot):
+        return (g_view, u_view)[a](slot) if a < 2 else d_view(slot, (a - 2) * BLOCK, BLOCK)
+
+    def owned(a):
+        return (gate_w, up_w)[a].at[0] if a < 2 else down_w.at[0, pl.ds((a - 2) * BLOCK, BLOCK)]
 
     def hop(way, step, a):
         slots = (LEFT, RIGHT)[way]
-        target = (right, left)[way]
-        sems = ag_s.at[way, step - 1, a], ag_r.at[way, step - 1, a]
-        if step == 4 and a == 2:
-            src, dst = d_half(slots[3], way), d_half(FAR, way)
-        elif step == 1:
-            src, dst = args[a], views[a](slots[1])
+        if step == 4 and a >= 2:
+            start = (a - 2) * BLOCK + way * BLOCK // 2
+            src, dst = d_view(slots[3], start, BLOCK // 2), d_view(FAR, start, BLOCK // 2)
         else:
-            src, dst = views[a](slots[step - 1]), views[a](slots[step])
-        return remote(src, dst, *sems, target, s)
+            src = owned(a) if step == 1 else view(a, slots[step - 1])
+            dst = view(a, slots[step])
+        return remote(src, dst, ag_s.at[way, step - 1, a], ag_r.at[way, step - 1, a], (right, left)[way], s)
 
     hops = []
 
     def send(step, a):
         for way in range(2):
-            if step == 4 and a < 2 and a != way:
-                continue
             cp = hop(way, step, a)
             cp.start()
             hops.append(cp)
@@ -121,7 +120,7 @@
     def forward(step, a):
         for way in range(2):
             hop(way, step, a).wait_recv()
-            if step < 3 or a == 2 or a == way:
+            if step < 3 or a >= 2 or a == way:
                 cp = hop(way, step + 1, a)
                 cp.start()
                 hops.append(cp)
@@ -133,7 +132,7 @@
     send(1, 0)
     send(1, 1)
     locals_ = [
-        pltpu.make_async_copy(args[a], views[a](OWN), local_sem.at[a]) for a in range(3)
+        pltpu.make_async_copy(owned(a), view(a, OWN), local_sem.at[a]) for a in range(2 + BLOCKS)
     ]
     for cp in locals_:
         cp.start()
@@ -175,18 +174,22 @@
 
     m = mixed[...]
     scale = lax.rsqrt(jnp.mean(m * m, axis=1, keepdims=True) + EPS)
-    normed[...] = (m * scale * gain[...].astype(F32)).astype(BF16)
-    one_c = idc[...] == iota((TOK, EXPERTS), 1)
-    one_r = idr[...] == iota((EXPERTS, TOK), 0)
-    fc, fr = one_c.astype(F32), one_r.astype(F32)
+    normed[...] = (m * scale * gain[...].reshape(1, D).astype(F32)).astype(BF16)
+    same = (iota((TOK, TOK), 0) == iota((TOK, TOK), 1)).astype(F32)
+    idr = ids[...].astype(F32)
+    idc = jnp.sum(same * idr, axis=1, keepdims=True)
+    capr = limits[...].astype(F32)
+    capc = jnp.sum(same[:EXPERTS, :EXPERTS] * capr, axis=1, keepdims=True)
+    fc = (idc == iota((TOK, EXPERTS), 1).astype(F32)).astype(F32)
+    fr = (idr == iota((EXPERTS, TOK), 0).astype(F32)).astype(F32)
     up_tri = (iota((TOK, TOK), 0) < iota((TOK, TOK), 1)).astype(F32).astype(BF16)
     lo_tri = (iota((TOK, TOK), 0) > iota((TOK, TOK), 1)).astype(F32).astype(BF16)
     rank_c = jnp.sum(dot(lo_tri, fc.astype(BF16)) * fc, axis=1, keepdims=True)
     rank_r = jnp.sum(dot(fr.astype(BF16), up_tri) * fr, axis=0, keepdims=True)
-    cap_c = jnp.sum(fc * capr[...].astype(F32), axis=1, keepdims=True)
-    cap_r = jnp.sum(fr * capc[...].astype(F32), axis=0, keepdims=True)
-    slot_c = jnp.where(rank_c < cap_c, idc[...].astype(F32) * CAP + rank_c, -1.0)
-    slot_r = jnp.where(rank_r < cap_r, idr[...].astype(F32) * CAP + rank_r, -1.0)
+    cap_c = jnp.sum(fc * capr, axis=1, keepdims=True)
+    cap_r = jnp.sum(fr * capc, axis=0, keepdims=True)
+    slot_c = jnp.where(rank_c < cap_c, idc * CAP + rank_c, -1.0)
+    slot_r = jnp.where(rank_r < cap_r, idr * CAP + rank_r, -1.0)
     sel[...] = (slot_c == iota((TOK, SLOTS), 1).astype(F32)).astype(F32).astype(BF16)
     sel_t = (slot_r == iota((SLOTS, TOK), 0).astype(F32)).astype(F32).astype(BF16)
     chosen = jnp.sum(dot_nt(normed[...], router[...]) * fc, axis=1, keepdims=True)
@@ -201,7 +204,7 @@
     def home(dh):
         return ((lo, 0), (0, 1 + lo), (1 - lo, 3), (1, 1 + lo))[dh]
 
-    for dh in (2, 1, 3, 0):
+    for dh in (0, 1, 3, 2):
         home_lo, kind = home(dh)
         to_h = lax.rem(h + dh, NH)
 
@@ -218,10 +221,6 @@
         lax.fori_loop(1 if dh == 0 else 0, NX * NC, to, 0)
     rows[pl.ds(aligned(place), CAP)] = packed[pl.ds(aligned(s * CAP), CAP)]
 
-    send(1, 2)
-    forward(1, 0)
-    forward(1, 1)
-
     ex = []
 
     def exchange(kind):
@@ -234,72 +233,71 @@
         cp.start()
         ex.append(cp)
 
+    def units(blocks, *slots):
+        for slot in slots:
+            for k in blocks:
+                r = pl.ds(k * HALF_ROWS, HALF_ROWS)
+                v = dot(rows[r], gu[slot])
+                g, u = v[:, :PIECE], v[:, PIECE:]
+                act[r, pl.ds(slot * PIECE, PIECE)] = (g / (1.0 + jnp.exp(-g)) * u).astype(BF16)
+
+    forward(1, 0)
+    forward(1, 1)
     exchange(0)
-    forward(1, 2)
+    send(1, 2)
     forward(2, 0)
     forward(2, 1)
+    forward(1, 2)
     exchange(1)
     exchange(2)
     exchange(3)
-    forward(2, 2)
     for cp in locals_:
         cp.wait()
-
-    def units(slot):
-        def body(i, _):
-            r = pl.ds(pl.multiple_of(i * 256, 256), 256)
-            v = dot(rows[r], gu[slot])
-            g, u = v[:, :PIECE], v[:, PIECE:]
-            act[r, pl.ds(slot * PIECE, PIECE)] = (g / (1.0 + jnp.exp(-g)) * u).astype(BF16)
-            return 0
-
-        lax.fori_loop(0, 2 * SLOTS // 256, body, 0)
-
-    for cp in ex:
-        cp.wait_recv()
-    units(0)
     forward(3, 0)
     forward(3, 1)
-    for slot in (1, 4, 2, 5, 3, 6):
-        units(slot)
+    forward(2, 2)
+    send(1, 3)
+    units((0, 1), 0, 1, 4, 2, 5)
     forward(3, 2)
+    forward(1, 3)
+    send(1, 4)
+    units((0, 1), 3, 6)
     hop(0, 4, 0).wait_recv()
     hop(1, 4, 1).wait_recv()
-    units(7)
-    hop(0, 4, 2).wait_recv()
-    hop(1, 4, 2).wait_recv()
-
-    px = []
-    for j in range(PARTS):
-        def down(i, _, j=j):
-            r = pl.ds(pl.multiple_of(i * 256, 256), 256)
-            r2 = pl.ds(pl.multiple_of(SLOTS + i * 256, 256), 256)
-            ps[j, r] = dot_nt(act[r2], wd[pl.ds(j * FEAT, FEAT)]).astype(BF16)
-            return 0
-
-        lax.fori_loop(0, SLOTS // 256, down, 0)
-        cp = remote(ps.at[j], pr.at[j], px_s.at[j], px_r.at[j], pair, s)
-        cp.start()
-        px.append(cp)
-
-    for j in range(PARTS):
-        def down_own(i, _, j=j):
-            r = pl.ds(pl.multiple_of(i * 256, 256), 256)
-            mine[j, r] = dot_nt(act[r], wd[pl.ds(j * FEAT, FEAT)])
-            return 0
-
-        lax.fori_loop(0, SLOTS // 256, down_own, 0)
-
-    for j in range(PARTS):
-        px[j].wait_recv()
-        bs[j] = (mine[j] + pr[j].astype(F32)).astype(BF16)
-        near = lax.rem(h + NH - 1 + 2 * lo, NH)
-        for kind in (3, 1, 2, 0):
+    forward(2, 3)
+    forward(1, 4)
+    send(1, 5)
+    units((0, 1), 7)
+    ex[0].wait_recv()
+    ex[1].wait_recv()
+    units((2,), 0, 1, 4, 2, 5, 3, 6, 7)
+    ex[2].wait_recv()
+    ex[3].wait_recv()
+    units((3,), 0, 1, 4, 2, 5, 3, 6, 7)
+
+    order = [(j, i) for j in range(PARTS) for i in (1, 0)]
+
+    def down(k, j):
+        return dot_nt(act[pl.ds(k * HALF_ROWS, HALF_ROWS)], wd[pl.ds(j * FEAT, FEAT)])
+
+    def part_of(ref, j, i):
+        return ref.at[j, pl.ds(i * HALF_ROWS, HALF_ROWS)]
+
+    px = [
+        remote(part_of(ps, j, i), part_of(pr, j, i), px_s.at[n], px_r.at[n], pair, s)
+        for n, (j, i) in enumerate(order)
+    ]
+    near = lax.rem(h + NH - 1 + 2 * lo, NH)
+
+    def give(j, i):
+        r = pl.ds(i * HALF_ROWS, HALF_ROWS)
+        bs[j, r] = (mine[j, r] + pr[j, r].astype(F32)).astype(BF16)
+        for kind in ((1, 0), (3, 2))[i]:
             to_h = (h, near, near, lax.rem(h + 2, NH))[kind]
             to_lo = (lo, 0, 1, 1 - lo)[kind]
 
-            def back(i, _, kind=kind, to_h=to_h, to_lo=to_lo, j=j):
-                tx, tc = lax.rem(x + i // NC, NX), lax.rem(c + lax.rem(i, NC), NC)
+            def back(n, _, kind=kind, to_h=to_h, to_lo=to_lo):
+                tx, tc = lax.rem(x + n // NC, NX), lax.rem(c + lax.rem(n, NC), NC)
                 t = (tx * NH + to_h) * NC + tc
                 remote(
                     bs.at[j, pl.ds(aligned(kind * GROUP + (tx * NC + tc) * CAP), CAP)],
@@ -309,7 +307,30 @@
                 return 0
 
             lax.fori_loop(1 if kind == 0 else 0, NX * NC, back, 0)
-        bk[j, pl.ds(aligned(s * CAP), CAP)] = bs[j, pl.ds(aligned(place), CAP)]
+        if i == 0:
+            bk[j, pl.ds(aligned(s * CAP), CAP)] = bs[j, pl.ds(aligned(place), CAP)]
+
+    def arrived(a):
+        for way in range(2):
+            hop(way, 4, a).wait_recv()
+
+    passing = {0: ((3, 3), (2, 4), (1, 5)), 1: ((3, 4), (2, 5)), 2: ((3, 5),)}
+    for n, (j, i) in enumerate(order):
+        if n % 2 == 0:
+            arrived(2 + j * BLOCKS // PARTS)
+        r = pl.ds(i * HALF_ROWS, HALF_ROWS)
+        ps[j, r] = down(2 + i, j).astype(BF16)
+        if n >= AHEAD:
+            px[n - AHEAD].wait_recv()
+        px[n].start()
+        mine[j, r] = down(i, j)
+        if n >= AHEAD:
+            give(*order[n - AHEAD])
+        for step, a in passing.get(n, ()):
+            forward(step, a)
+    for n in range(len(order) - AHEAD, len(order)):
+        px[n].wait_recv()
+        give(*order[n])
 
     for j in range(PARTS):
         block = bk.at[j, pl.ds(0, SLOTS - CAP)]
@@ -335,7 +356,7 @@
     return pl.pallas_call(
         layer,
         out_shape=jax.ShapeDtypeStruct((1, TOK, D), BF16),
-        in_specs=[vmem] * 8 + [anywhere] * 3,
+        in_specs=[vmem] * 6 + [anywhere] * 3,
         out_specs=vmem,
         scratch_shapes=[
             pltpu.VMEM((TOK + 4 * CAP, D), BF16),
@@ -354,12 +375,12 @@
             pltpu.VMEM((PARTS, SLOTS, FEAT), F32),
             pltpu.VMEM((PARTS, SLOTS, FEAT), BF16),
             pltpu.VMEM((PARTS, SLOTS, FEAT), BF16),
-            dma((3,)),
+            dma((2 + BLOCKS,)),
             dma((2,)), dma((2,)),
-            dma((2, 4, 3)), dma((2, 4, 3)),
+            dma((2, 4, 2 + BLOCKS)), dma((2, 4, 2 + BLOCKS)),
             dma, dma((4,)),
             dma((4,)), dma((4,)),
-            dma((PARTS,)), dma((PARTS,)),
+            dma((2 * PARTS,)), dma((2 * PARTS,)),
             dma((PARTS,)), dma((PARTS,)),
         ],
         compiler_params=pltpu.CompilerParams(
@@ -367,12 +388,10 @@
         ),
     )(
         tokens,
-        expert_ids.reshape(TOK, 1),
         expert_ids.reshape(1, TOK),
-        expert_capacity.reshape(EXPERTS, 1),
         expert_capacity.reshape(1, EXPERTS),
         kernel_weight.T,
-        norm_gain.reshape(1, D),
+        norm_gain,
         router.T,
         expert_gate,
         expert_up,

time: 128 us -> 117 us (0.914)
  Pallas kernels: 122 us -> 115 us
  local copies, waits for them, and re-layouts: 4.7 us -> 1.87 us
    pallas_call x1, Pallas kernels: 122 us -> 115 us  [on_device(): pl.pallas_call(layer, out_shape=jax.ShapeDtypeStruct((1, TOK, D), BF16),...]
    reshape x3 -> x0, local copies, waits for them, and re-layouts: 2.08 us -> none  [the longest x1 0.8 us: on_device(): expert_ids.reshape(TOK, 1)]
    unnamed x7 -> x1, local copies, waits for them, and re-layouts: 2.61 us -> 1.87 us
where the time goes in v2:
time: 117 us
  Pallas kernels  115 us (98%)
  local copies, waits for them, and re-layouts  1.87 us (2%)
    pallas_call x1, Pallas kernels, on_device(): pl.pallas_call(layer, out_shape=jax.ShapeDtypeStruct((1, TOK, D), BF16),...  115 us

profile of v2, /device:TPU:1, one launch (start us, length us, event | category | flops | bytes accessed | tf_op | source)
XLA Modules:
  0.0 117.0 jit_solution(12923648074785243833)
XLA Ops:
  0.0 115.2 %shard_map.91 = bf16[1,256,1024]{2,1,0:T(8,128)(2,1)} custom-call(bf16[1,256,1024]{2,1,0:T(8,128)(2,1)} %tokens.1, s32[1,256]{1,0:T(1,128)} %bitcast.6, s32[1,32]{1,0:T(1,128)} %bitcast.7, bf16[496,1024]{1,0:T(8,128)(2,1)} %bitcast.4, bf16[1024]{0:T(1024)(128)(2,1)} %gain.1, bf16[32,1024]{1,0:T(8,128)(2,1)} %bitcast.5, bf16[1,1024,128]{2,1,0:T(8,128)(2,1)} %gate_w.1, ...), custom_call_target="tpu_custom_call" | custom-call | tf_op jit(solution)/shard_map/pallas_call | solution.py:356
  115.2 1.9 %copy.11 = bf16[1,256,1024]{2,1,0:T(8,128)(2,1)} copy(bf16[1,256,1024]{2,1,0:T(8,128)(2,1)} %shard_map.91) | data formatting | bytes 1048576

commit v3 on v2

--- a/solution.py
+++ b/solution.py
@@ -22,7 +22,7 @@
 EPS = 1e-06
 
 NX, NH, NC, NY = 4, 4, 2, 8
-GROUP = NX * NC * CAP
+GROUP = NH * NC * CAP
 PIECE = 128
 PARTS = 4
 FEAT = D // PARTS
@@ -51,9 +51,9 @@
 def layer(
     tokens, ids, limits, kwt, gain, router, gate_w, up_w, down_w,
     out,
-    xp, pt, mixed, normed, packed, sel, gate_s,
+    xp, kw_in, pt, mixed, normed, packed, sel, gate_s,
     rows, gu, wd, act, ps, pr, mine, bs, bk,
-    local_sem, halo_s, halo_r, ag_s, ag_r, fwd_s, fwd_r, ex_s, ex_r, px_s, px_r, ret_s, ret_r,
+    in_sem, local_sem, halo_s, halo_r, ag_s, ag_r, fwd_s, fwd_r, ex_s, ex_r, px_s, px_r, ret_s, ret_r,
 ):
     s = lax.axis_index("seq")
     b = lax.axis_index("blk")
@@ -66,6 +66,14 @@
     pair = (1 - lo) * NY + y
     seqs = NX * NH * NC
 
+    here = pl.ds(CAP, TOK)
+    inputs = [
+        pltpu.make_async_copy(tokens.at[0], xp.at[here], in_sem.at[0]),
+        pltpu.make_async_copy(kwt, kw_in, in_sem.at[1]),
+    ]
+    for cp in inputs:
+        cp.start()
+
     barrier = pltpu.get_barrier_semaphore()
 
     for dh, to_lo in ((0, lo), (1, lo), (3, lo), (3 - 2 * lo, 1 - lo), (2, 1 - lo)):
@@ -137,14 +145,15 @@
     for cp in locals_:
         cp.start()
 
-    xp[pl.ds(CAP, TOK)] = tokens[0]
     xp[pl.ds(TOK + 2 * CAP, 32)] = jnp.zeros((32, D), BF16)
     row, col = iota((512, HEADS * TAPS), 0), iota((512, HEADS * TAPS), 1)
     tap = row & 31
     spread = ((col == (row >> 5) * TAPS + tap) & (tap < TAPS)).astype(F32).astype(BF16)
-    kw = dot(spread, kwt[...]).astype(BF16)
+    for cp in inputs:
+        cp.wait()
+    kw = dot(spread, kw_in[...]).astype(BF16)
     for q in range(4):
-        logits = dot_nt(kw[q * 128 : (q + 1) * 128], tokens[0]).reshape(4, 32, TOK)
+        logits = dot_nt(kw[q * 128 : (q + 1) * 128], xp[here]).reshape(4, 32, TOK)
         logits = jnp.where(iota(logits.shape, 1) < TAPS, logits, -3e38)
         e = jnp.exp(logits - jnp.max(logits, axis=1, keepdims=True))
         p = e / jnp.sum(e, axis=1, keepdims=True)
@@ -170,7 +179,7 @@
                 cols = pl.ds((2 * q + i) * 128, 128)
                 window = xp[pl.ds(t * 64, 128), cols]
                 conv = jnp.where(lane < 64, dot(bands[2 * i], window), dot(bands[2 * i + 1], window))
-                mixed[pl.ds(t * 64, 64), cols] = conv + tokens[0, pl.ds(t * 64, 64), cols].astype(F32)
+                mixed[pl.ds(t * 64, 64), cols] = conv + xp[pl.ds(CAP + t * 64, 64), cols].astype(F32)
 
     m = mixed[...]
     scale = lax.rsqrt(jnp.mean(m * m, axis=1, keepdims=True) + EPS)
@@ -196,30 +205,31 @@
     gate_s[...] = 1.0 / (1.0 + jnp.exp(-chosen))
     packed[...] = dot(sel_t, normed[...]).astype(BF16)
 
-    place = (x * NC + c) * CAP
-
     def aligned(v):
         return pl.multiple_of(v, CAP)
 
+    def place(dx, kind, core):
+        return aligned(dx * GROUP + (kind * NC + core) * CAP)
+
     def home(dh):
         return ((lo, 0), (0, 1 + lo), (1 - lo, 3), (1, 1 + lo))[dh]
 
-    for dh in (0, 1, 3, 2):
-        home_lo, kind = home(dh)
-        to_h = lax.rem(h + dh, NH)
-
-        def to(i, _, home_lo=home_lo, kind=kind, to_h=to_h):
-            tx, tc = lax.rem(x + i // NC, NX), lax.rem(c + lax.rem(i, NC), NC)
-            e = (tx * NH + to_h) * NC + tc
-            remote(
-                packed.at[pl.ds(aligned(e * CAP), CAP)],
-                rows.at[pl.ds(aligned(kind * GROUP + place), CAP)],
-                fwd_s, fwd_r.at[kind], home_lo * NY + y, e,
-            ).start()
+    for dx in range(NX):
+        def to(n, _, dx=dx, turns=(2, 1, 3, 0)):
+            for dh in turns:
+                home_lo, kind = home(dh)
+                e = (lax.rem(x + dx, NX) * NH + lax.rem(h + dh, NH)) * NC + lax.rem(c + n, NC)
+                remote(
+                    packed.at[pl.ds(aligned(e * CAP), CAP)],
+                    rows.at[pl.ds(place(dx, kind, c), CAP)],
+                    fwd_s, fwd_r.at[dx], home_lo * NY + y, e,
+                ).start()
             return 0
 
-        lax.fori_loop(1 if dh == 0 else 0, NX * NC, to, 0)
-    rows[pl.ds(aligned(place), CAP)] = packed[pl.ds(aligned(s * CAP), CAP)]
+        if dx == 0:
+            to(0, 0, turns=(2, 1, 3))
+        lax.fori_loop(1 if dx == 0 else 0, NC, to, 0)
+    rows[pl.ds(place(0, 0, c), CAP)] = packed[pl.ds(aligned(s * CAP), CAP)]
 
     ex = []
 
@@ -243,37 +253,36 @@
 
     forward(1, 0)
     forward(1, 1)
+    send(1, 2)
     exchange(0)
-    send(1, 2)
+    for cp in locals_:
+        cp.wait()
     forward(2, 0)
     forward(2, 1)
     forward(1, 2)
     exchange(1)
+    units((0,), 0, 1, 4, 2, 5)
     exchange(2)
     exchange(3)
-    for cp in locals_:
-        cp.wait()
     forward(3, 0)
     forward(3, 1)
     forward(2, 2)
+    units((1,), 0, 1, 4, 2, 5)
+    units((0, 1), 3, 6)
+    forward(3, 2)
     send(1, 3)
-    units((0, 1), 0, 1, 4, 2, 5)
-    forward(3, 2)
-    forward(1, 3)
+    ex[0].wait_recv()
+    ex[1].wait_recv()
+    units((2,), 0, 1, 4, 2, 5, 3, 6)
     send(1, 4)
-    units((0, 1), 3, 6)
+    ex[2].wait_recv()
+    ex[3].wait_recv()
+    units((3,), 0, 1, 4, 2, 5, 3, 6)
     hop(0, 4, 0).wait_recv()
     hop(1, 4, 1).wait_recv()
-    forward(2, 3)
-    forward(1, 4)
+    forward(1, 3)
     send(1, 5)
-    units((0, 1), 7)
-    ex[0].wait_recv()
-    ex[1].wait_recv()
-    units((2,), 0, 1, 4, 2, 5, 3, 6, 7)
-    ex[2].wait_recv()
-    ex[3].wait_recv()
-    units((3,), 0, 1, 4, 2, 5, 3, 6, 7)
+    units((3, 1, 2, 0), 7)
 
     order = [(j, i) for j in range(PARTS) for i in (1, 0)]
 
@@ -292,29 +301,30 @@
     def give(j, i):
         r = pl.ds(i * HALF_ROWS, HALF_ROWS)
         bs[j, r] = (mine[j, r] + pr[j, r].astype(F32)).astype(BF16)
-        for kind in ((1, 0), (3, 2))[i]:
-            to_h = (h, near, near, lax.rem(h + 2, NH))[kind]
-            to_lo = (lo, 0, 1, 1 - lo)[kind]
-
-            def back(n, _, kind=kind, to_h=to_h, to_lo=to_lo):
-                tx, tc = lax.rem(x + n // NC, NX), lax.rem(c + lax.rem(n, NC), NC)
-                t = (tx * NH + to_h) * NC + tc
+
+        def back(n, _, kinds=(3, 1, 2, 0)):
+            dx, tc = 2 * i + n // NC, lax.rem(c + lax.rem(n, NC), NC)
+            for kind in kinds:
+                to_h = (h, near, near, lax.rem(h + 2, NH))[kind]
+                to_lo = (lo, 0, 1, 1 - lo)[kind]
+                t = (lax.rem(x + NX - dx, NX) * NH + to_h) * NC + tc
                 remote(
-                    bs.at[j, pl.ds(aligned(kind * GROUP + (tx * NC + tc) * CAP), CAP)],
+                    bs.at[j, pl.ds(place(dx, kind, tc), CAP)],
                     bk.at[j, pl.ds(aligned(s * CAP), CAP)],
                     ret_s.at[j], ret_r.at[j], to_lo * NY + y, t,
                 ).start()
-                return 0
-
-            lax.fori_loop(1 if kind == 0 else 0, NX * NC, back, 0)
+            return 0
+
         if i == 0:
-            bk[j, pl.ds(aligned(s * CAP), CAP)] = bs[j, pl.ds(aligned(place), CAP)]
+            back(0, 0, kinds=(3, 1, 2))
+            bk[j, pl.ds(aligned(s * CAP), CAP)] = bs[j, pl.ds(place(0, 0, c), CAP)]
+        lax.fori_loop(1 if i == 0 else 0, 2 * NC, back, 0)
 
     def arrived(a):
         for way in range(2):
             hop(way, 4, a).wait_recv()
 
-    passing = {0: ((3, 3), (2, 4), (1, 5)), 1: ((3, 4), (2, 5)), 2: ((3, 5),)}
+    passing = {0: ((2, 3), (1, 4)), 1: ((3, 3), (2, 4), (1, 5)), 2: ((3, 4), (2, 5)), 3: ((3, 5),)}
     for n, (j, i) in enumerate(order):
         if n % 2 == 0:
             arrived(2 + j * BLOCKS // PARTS)
@@ -356,10 +366,11 @@
     return pl.pallas_call(
         layer,
         out_shape=jax.ShapeDtypeStruct((1, TOK, D), BF16),
-        in_specs=[vmem] * 6 + [anywhere] * 3,
+        in_specs=[anywhere, vmem, vmem, anywhere, vmem, vmem] + [anywhere] * 3,
         out_specs=vmem,
         scratch_shapes=[
             pltpu.VMEM((TOK + 4 * CAP, D), BF16),
+            pltpu.VMEM((HEADS * TAPS, D), BF16),
             pltpu.VMEM((4, TOK, 128), F32),
             pltpu.VMEM((TOK, D), F32),
             pltpu.VMEM((TOK, D), BF16),
@@ -375,6 +386,7 @@
             pltpu.VMEM((PARTS, SLOTS, FEAT), F32),
             pltpu.VMEM((PARTS, SLOTS, FEAT), BF16),
             pltpu.VMEM((PARTS, SLOTS, FEAT), BF16),
+            dma((2,)),
             dma((2 + BLOCKS,)),
             dma((2,)), dma((2,)),
             dma((2, 4, 2 + BLOCKS)), dma((2, 4, 2 + BLOCKS)),

time: 117 us -> 113 us (0.966)
  Pallas kernels: 115 us -> 111 us
    pallas_call x1, Pallas kernels: 115 us -> 111 us  [on_device(): pl.pallas_call(layer, out_shape=jax.ShapeDtypeStruct((1, TOK, D), BF16),...]
where the time goes in v3:
time: 113 us
  Pallas kernels  111 us (98%)
  local copies, waits for them, and re-layouts  1.87 us (2%)
    pallas_call x1, Pallas kernels, on_device(): pl.pallas_call(layer, out_shape=jax.ShapeDtypeStruct((1, TOK, D), BF16),...  111 us

profile of v3, /device:TPU:1, one launch (start us, length us, event | category | flops | bytes accessed | tf_op | source)
XLA Modules:
  0.0 112.7 jit_solution(14030662477540530056)
XLA Ops:
  0.0 110.9 %shard_map.91 = bf16[1,256,1024]{2,1,0:T(8,128)(2,1)} custom-call(bf16[1,256,1024]{2,1,0:T(8,128)(2,1)} %tokens.1, s32[1,256]{1,0:T(1,128)} %bitcast.6, s32[1,32]{1,0:T(1,128)} %bitcast.7, bf16[496,1024]{1,0:T(8,128)(2,1)} %bitcast.4, bf16[1024]{0:T(1024)(128)(2,1)} %gain.1, bf16[32,1024]{1,0:T(8,128)(2,1)} %bitcast.5, bf16[1,1024,128]{2,1,0:T(8,128)(2,1)} %gate_w.1, ...), custom_call_target="tpu_custom_call" | custom-call | tf_op jit(solution)/shard_map/pallas_call | solution.py:366
  110.9 1.9 %copy.11 = bf16[1,256,1024]{2,1,0:T(8,128)(2,1)} copy(bf16[1,256,1024]{2,1,0:T(8,128)(2,1)} %shard_map.91) | data formatting | bytes 1048576

commit v4 on v3

--- a/solution.py
+++ b/solution.py
@@ -139,6 +139,7 @@
     head.start()
     send(1, 0)
     send(1, 1)
+    send(1, 2)
     locals_ = [
         pltpu.make_async_copy(owned(a), view(a, OWN), local_sem.at[a]) for a in range(2 + BLOCKS)
     ]
@@ -253,34 +254,34 @@
 
     forward(1, 0)
     forward(1, 1)
-    send(1, 2)
+    forward(1, 2)
     exchange(0)
     for cp in locals_:
         cp.wait()
     forward(2, 0)
     forward(2, 1)
-    forward(1, 2)
+    forward(2, 2)
+    send(1, 3)
     exchange(1)
     units((0,), 0, 1, 4, 2, 5)
     exchange(2)
     exchange(3)
     forward(3, 0)
     forward(3, 1)
-    forward(2, 2)
+    forward(3, 2)
+    forward(1, 3)
     units((1,), 0, 1, 4, 2, 5)
     units((0, 1), 3, 6)
-    forward(3, 2)
-    send(1, 3)
     ex[0].wait_recv()
     ex[1].wait_recv()
+    send(1, 4)
     units((2,), 0, 1, 4, 2, 5, 3, 6)
-    send(1, 4)
     ex[2].wait_recv()
     ex[3].wait_recv()
     units((3,), 0, 1, 4, 2, 5, 3, 6)
     hop(0, 4, 0).wait_recv()
     hop(1, 4, 1).wait_recv()
-    forward(1, 3)
+    forward(2, 3)
     send(1, 5)
     units((3, 1, 2, 0), 7)
 
@@ -324,7 +325,7 @@
         for way in range(2):
             hop(way, 4, a).wait_recv()
 
-    passing = {0: ((2, 3), (1, 4)), 1: ((3, 3), (2, 4), (1, 5)), 2: ((3, 4), (2, 5)), 3: ((3, 5),)}
+    passing = {0: ((3, 3), (1, 4)), 1: ((2, 4), (1, 5)), 2: ((3, 4), (2, 5)), 3: ((3, 5),)}
     for n, (j, i) in enumerate(order):
         if n % 2 == 0:
             arrived(2 + j * BLOCKS // PARTS)

time: 113 us -> 111 us (0.982)
  Pallas kernels: 111 us -> 109 us
    pallas_call x1, Pallas kernels: 111 us -> 109 us  [on_device(): pl.pallas_call(layer, out_shape=jax.ShapeDtypeStruct((1, TOK, D), BF16),...]
where the time goes in v4:
time: 111 us
  Pallas kernels  109 us (98%)
  local copies, waits for them, and re-layouts  1.87 us (2%)
    pallas_call x1, Pallas kernels, on_device(): pl.pallas_call(layer, out_shape=jax.ShapeDtypeStruct((1, TOK, D), BF16),...  109 us

profile of v4, /device:TPU:1, one launch (start us, length us, event | category | flops | bytes accessed | tf_op | source)
XLA Modules:
  0.0 110.7 jit_solution(892424051834761274)
XLA Ops:
  0.0 108.8 %shard_map.91 = bf16[1,256,1024]{2,1,0:T(8,128)(2,1)} custom-call(bf16[1,256,1024]{2,1,0:T(8,128)(2,1)} %tokens.1, s32[1,256]{1,0:T(1,128)} %bitcast.6, s32[1,32]{1,0:T(1,128)} %bitcast.7, bf16[496,1024]{1,0:T(8,128)(2,1)} %bitcast.4, bf16[1024]{0:T(1024)(128)(2,1)} %gain.1, bf16[32,1024]{1,0:T(8,128)(2,1)} %bitcast.5, bf16[1,1024,128]{2,1,0:T(8,128)(2,1)} %gate_w.1, ...), custom_call_target="tpu_custom_call" | custom-call | tf_op jit(solution)/shard_map/pallas_call | solution.py:367
  108.8 1.9 %copy.11 = bf16[1,256,1024]{2,1,0:T(8,128)(2,1)} copy(bf16[1,256,1024]{2,1,0:T(8,128)(2,1)} %shard_map.91) | data formatting | bytes 1048576

commit v5 on v4

--- a/solution.py
+++ b/solution.py
@@ -334,9 +334,9 @@
         if n >= AHEAD:
             px[n - AHEAD].wait_recv()
         px[n].start()
-        mine[j, r] = down(i, j)
         if n >= AHEAD:
             give(*order[n - AHEAD])
+        mine[j, r] = down(i, j)
         for step, a in passing.get(n, ()):
             forward(step, a)
     for n in range(len(order) - AHEAD, len(order)):

time: 111 us -> 110 us (level)
  no operation moved by 1% of the time
where the time goes in v5:
time: 110 us
  Pallas kernels  108 us (98%)
  local copies, waits for them, and re-layouts  1.87 us (2%)
    pallas_call x1, Pallas kernels, on_device(): pl.pallas_call(layer, out_shape=jax.ShapeDtypeStruct((1, TOK, D), BF16),...  108 us

profile of v5, /device:TPU:1, one launch (start us, length us, event | category | flops | bytes accessed | tf_op | source)
XLA Modules:
  0.0 110.3 jit_solution(11418946251777736190)
XLA Ops:
  0.0 108.4 %shard_map.91 = bf16[1,256,1024]{2,1,0:T(8,128)(2,1)} custom-call(bf16[1,256,1024]{2,1,0:T(8,128)(2,1)} %tokens.1, s32[1,256]{1,0:T(1,128)} %bitcast.6, s32[1,32]{1,0:T(1,128)} %bitcast.7, bf16[496,1024]{1,0:T(8,128)(2,1)} %bitcast.4, bf16[1024]{0:T(1024)(128)(2,1)} %gain.1, bf16[32,1024]{1,0:T(8,128)(2,1)} %bitcast.5, bf16[1,1024,128]{2,1,0:T(8,128)(2,1)} %gate_w.1, ...), custom_call_target="tpu_custom_call" | custom-call | tf_op jit(solution)/shard_map/pallas_call | solution.py:367
  108.4 1.9 %copy.11 = bf16[1,256,1024]{2,1,0:T(8,128)(2,1)} copy(bf16[1,256,1024]{2,1,0:T(8,128)(2,1)} %shard_map.91) | data formatting | bytes 1048576

commit v6 on v5

--- a/solution.py
+++ b/solution.py
@@ -327,14 +327,18 @@
 
     passing = {0: ((3, 3), (1, 4)), 1: ((2, 4), (1, 5)), 2: ((3, 4), (2, 5)), 3: ((3, 5),)}
     for n, (j, i) in enumerate(order):
-        if n % 2 == 0:
+        waits = n % 2 == 0
+        if n >= AHEAD and waits:
+            px[n - AHEAD].wait_recv()
+            give(*order[n - AHEAD])
+        if waits:
             arrived(2 + j * BLOCKS // PARTS)
         r = pl.ds(i * HALF_ROWS, HALF_ROWS)
         ps[j, r] = down(2 + i, j).astype(BF16)
-        if n >= AHEAD:
+        if n >= AHEAD and not waits:
             px[n - AHEAD].wait_recv()
         px[n].start()
-        if n >= AHEAD:
+        if n >= AHEAD and not waits:
             give(*order[n - AHEAD])
         mine[j, r] = down(i, j)
         for step, a in passing.get(n, ()):

time: 110 us -> 111 us (level)
  no operation moved by 1% of the time
where the time goes in v6:
time: 111 us; the launch traced here: 110 us
  Pallas kernels  109 us (98%)
  local copies, waits for them, and re-layouts  1.87 us (2%)
    pallas_call x1, Pallas kernels, on_device(): pl.pallas_call(layer, out_shape=jax.ShapeDtypeStruct((1, TOK, D), BF16),...  109 us

profile of v6, /device:TPU:1, one launch (start us, length us, event | category | flops | bytes accessed | tf_op | source)
XLA Modules:
  0.0 110.4 jit_solution(17111586787917143485)
XLA Ops:
  0.0 108.6 %shard_map.91 = bf16[1,256,1024]{2,1,0:T(8,128)(2,1)} custom-call(bf16[1,256,1024]{2,1,0:T(8,128)(2,1)} %tokens.1, s32[1,256]{1,0:T(1,128)} %bitcast.6, s32[1,32]{1,0:T(1,128)} %bitcast.7, bf16[496,1024]{1,0:T(8,128)(2,1)} %bitcast.4, bf16[1024]{0:T(1024)(128)(2,1)} %gain.1, bf16[32,1024]{1,0:T(8,128)(2,1)} %bitcast.5, bf16[1,1024,128]{2,1,0:T(8,128)(2,1)} %gate_w.1, ...), custom_call_target="tpu_custom_call" | custom-call | tf_op jit(solution)/shard_map/pallas_call | solution.py:371
  108.6 1.9 %copy.11 = bf16[1,256,1024]{2,1,0:T(8,128)(2,1)} copy(bf16[1,256,1024]{2,1,0:T(8,128)(2,1)} %shard_map.91) | data formatting | bytes 1048576
